TPU v7x, 32 devices: a whole 2x2x4 slice. The times are simulated.
32 devices in a mesh: gx: 16 (over z, y, core), gy: 2 (over x).
Axes of the slice: x: 2, y: 2, z: 4, core: 2. Of those that a mesh axis runs over, the one named last changes fastest.
Arguments:
- planes: bfloat16 [3, 64, 128, 128], P(None, 'gx', 'gy'), may hold values from -6 to 6
- kernel: bfloat16 [3, 3, 3, 16, 128], replicated, may hold values from -0.3125 to 0.3125
- bias: float32 [128], replicated, may hold values from -4 to 4
- cotangent: bfloat16 [64, 128, 128], P('gx', 'gy'), may hold values from -6 to 6
Outputs:
- output: bfloat16 [64, 128, 128], P('gx', 'gy')
- input_grad: bfloat16 [3, 64, 128, 128], P(None, 'gx', 'gy')
- kernel_grad: float32 [3, 3, 3, 16, 128], replicated
- bias_grad: float32 [128], replicated
All inputs are finite; a program needn't handle non-finite values.
Results may differ from a plain program's by a relative error of at most 0.001.
Values may be sent and summed in bfloat16 or wider, within the bound.
A program may use at most 64 MiB of HBM per device.

v0:
```python
import jax
import jax.numpy as jnp
from jax import lax
from jax.sharding import PartitionSpec as P

GROUPS = 8


def padded_2(array, sides, width):
    for axis, dim in sides:
        count, length = (lax.axis_size(axis), array.shape[dim])
        up = [(i, (i + 1) % count) for i in range(count)]
        down = [(j, i) for i, j in up]
        last = lax.slice_in_dim(array, length - width, length, axis=dim)
        initial = lax.slice_in_dim(array, 0, width, axis=dim)
        before = lax.ppermute(last, axis, up)
        after = lax.ppermute(initial, axis, down)
        array = jnp.concatenate([before, array, after], axis=dim)
    return array


def shards(planes, kernel, bias, cotangent):
    width_x = planes.shape[1]
    width_y = planes.shape[2]
    channels = planes.shape[3]
    groups = GROUPS
    group_width = channels // groups
    cells = width_x * width_y
    padded = padded_2(planes, (("gx", 1), ("gy", 2)), 1)
    slope_pad = padded_2(cotangent, (("gx", 0), ("gy", 1)), 1)
    block_mask = jnp.eye(groups, dtype=kernel.dtype)
    block_mask_f = jnp.eye(groups, dtype=jnp.float32)
    slope_rows = cotangent.reshape(cells, channels)
    forward = jnp.zeros((cells, channels), jnp.float32)
    backward = []
    kernel_rows = []
    for depth in range(3):
        grad_plane = jnp.zeros((cells, channels), jnp.float32)
        for tap_x in range(3):
            for tap_y in range(3):
                tap_w = kernel[depth, tap_x, tap_y].reshape(group_width, groups, group_width)
                dense_w = (block_mask[:, None, :, None] * tap_w[None, :, :, :]).reshape(
                    channels, channels
                )
                moved = padded[depth, tap_x : tap_x + width_x, tap_y : tap_y + width_y, :].reshape(
                    cells, channels
                )
                forward = forward + jnp.dot(moved, dense_w, preferred_element_type=jnp.float32)
                back_slope = slope_pad[
                    2 - tap_x : 2 - tap_x + width_x, 2 - tap_y : 2 - tap_y + width_y, :
                ].reshape(cells, channels)
                grad_plane = grad_plane + lax.dot_general(
                    back_slope,
                    dense_w,
                    (((1,), (1,)), ((), ())),
                    preferred_element_type=jnp.float32,
                )
                full_grad = lax.dot_general(
                    moved, slope_rows, (((0,), (0,)), ((), ())), preferred_element_type=jnp.float32
                )
                full_grad = full_grad.reshape(groups, group_width, groups, group_width)
                diagonal = jnp.sum(full_grad * block_mask_f[:, None, :, None], axis=0)
                kernel_rows.append(diagonal.reshape(group_width, channels))
        backward.append(grad_plane.reshape(width_x, width_y, channels))
    output = (forward.reshape(width_x, width_y, channels) + bias).astype(jnp.bfloat16)
    input_grad = jnp.stack(backward).astype(jnp.bfloat16)
    kernel_part = jnp.stack(kernel_rows).reshape(3, 3, 3, group_width, channels)
    bias_part = jnp.sum(cotangent.astype(jnp.float32), axis=(0, 1))
    kernel_sum, bias_sum = lax.psum((kernel_part, bias_part), ("gx", "gy"))
    total_cells = cells * lax.axis_size("gx") * lax.axis_size("gy")
    scale = 1.0 / jnp.sqrt(jnp.float32(total_cells))
    return (output, input_grad, kernel_sum * scale, bias_sum * scale)


def solution(mesh):
    in_specs = (P(None, "gx", "gy", None), P(), P(), P("gx", "gy", None))
    out_specs = (P("gx", "gy", None), P(None, "gx", "gy", None), P(), P())
    return jax.shard_map(shards, mesh=mesh, in_specs=in_specs, out_specs=out_specs, check_vma=False)
```

profile of v0, /device:TPU:0, one launch (start us, length us, event | category | flops | bytes accessed | tf_op | source)
XLA Modules:
  0.0 298.1 jit_solution(8972012914744034552)
XLA Ops:
  7.2 1.5 fusion.85
  9.2 5.0 %collective-permute-start.1 = (bf16[3,1,64,128]{3,2,1,0:T(8,128)(2,1)}, bf16[3,1,64,128]{3,2,1,0:T(8,128)(2,1)}, u32[]{:S(2)}, u32[]{:S(2)}) collective-permute-start(bf16[3,1,64,128]{3,2,1,0:T(8,128)(2,1)} %get-tuple-element.36), channel_id=1, source_target_pairs={{2,0},{4,2},{6,4},{8,6},{10,8},{12,10},{14,12},{16,14},{18,16},{20... | collective-permute-start | bytes 147464 | tf_op jit(solution)/shard_map/ppermute | solution.py:17
  18.8 0.8 convolution_bitcast_fusion
  32.0 2.9 broadcast_multiply_fusion.3
  35.0 1.8 mul.1067
  36.8 0.7 copy.109
  37.5 1.6 convolution_bitcast_fusion.1
  40.7 0.9 fusion.4
  41.6 0.9 fusion.13
  42.4 38.9 %psum.15 = f32[128]{0:T(128)S(1)} all-reduce(f32[128]{0:T(128)S(1)} %copy-done.71), channel_id=1, replica_groups=mesh['gx'=16,'gy'=2] {'gx','gy'}, use_global_device_ids=true, to_apply=%region_29.0 | all-reduce | flops 128 | bytes 1024 | tf_op jit(solution)/shard_map/psum | solution.py:69
  81.8 0.9 fusion.22
  95.2 0.8 pad_maximum_fusion.4
  95.9 2.3 collective-permute-start.6
  99.8 2.0 collective-permute-done.7
  108.0 0.8 constant_dynamic-update-slice_fusion.4
  109.3 0.8 constant_dynamic-update-slice_fusion.5
  111.7 1.9 collective-permute-start.2
  118.5 0.7 copy.87
  121.9 0.7 copy.99
  125.5 0.7 copy.117
  129.8 1.1 fusion.2
  131.0 1.1 fusion.3
  132.7 1.1 fusion.6
  134.5 1.1 fusion.8
  136.3 1.1 fusion.9
  139.2 1.1 fusion.12
  142.3 1.1 fusion.15
  144.1 1.1 fusion.17
  145.9 1.1 fusion.18
  148.8 1.1 fusion.21
  171.3 118.3 %all-reduce.2.cloned.1.call-done = f32[3,3,3,16,128]{4,3,2,1,0:T(8,128)} async-done(((f32[3,3,3,16,128]{4,3,2,1,0:T(8,128)}), f32[3,3,3,16,128]{4,3,2,1,0:T(8,128)}) %all-reduce.2.cloned.1.call-update) | async-done | bytes 221200 | tf_op jit(solution)/shard_map/psum | solution.py:69
  289.6 1.6 broadcast_multiply_fusion.27
  (403 shorter events, 85.0 us)
Async XLA Ops:
  7.2 7.1 %copy-start = (bf16[4,64,128]{2,1,0:T(8,128)(2,1)S(1)}, bf16[4,64,128]{2,1,0:T(8,128)(2,1)}, u32[]{:S(2)}) copy-start(bf16[4,64,128]{2,1,0:T(8,128)(2,1)} %param.7) | copy-start | bytes 196612
  7.2 8.3 %copy-start.37 = (bf16[3,3,3,16,128]{4,3,2,1,0:T(8,128)(2,1)S(1)}, bf16[3,3,3,16,128]{4,3,2,1,0:T(8,128)(2,1)}, u32[]{:S(2)}) copy-start(bf16[3,3,3,16,128]{4,3,2,1,0:T(8,128)(2,1)} %param.5) | copy-start | bytes 331780
  7.2 282.4 %all-reduce.2.cloned.1.call-start = ((), (), s32[]{:S(2)}) async-start(), calls=%async_computation | async-start | bytes 442368 | tf_op jit(solution)/shard_map/psum | solution.py:69
  8.7 6.8 %copy-start.1 = (bf16[3,4,64,128]{3,2,1,0:T(8,128)(2,1)S(1)}, bf16[3,4,64,128]{3,2,1,0:T(8,128)(2,1)}, u32[]{:S(2)}) copy-start(bf16[3,4,64,128]{3,2,1,0:T(8,128)(2,1)} %param.4) | copy-start | bytes 589828
  8.7 99.3 %collective-permute-start = (bf16[3,1,64,128]{3,2,1,0:T(8,128)(2,1)}, bf16[3,1,64,128]{3,2,1,0:T(8,128)(2,1)}, u32[]{:S(2)}, u32[]{:S(2)}) collective-permute-start(bf16[3,1,64,128]{3,2,1,0:T(8,128)(2,1)} %get-tuple-element.37), channel_id=1, source_target_pairs={{0,2},{2,4},{4,6},{6,8},{8,10},{10,12},{12,14},{14,16},{16,18},{18... | collective-permute-start | bytes 147464 | tf_op jit(solution)/shard_map/ppermute | solution.py:16
  9.2 100.1 %collective-permute-start.1 = (bf16[3,1,64,128]{3,2,1,0:T(8,128)(2,1)}, bf16[3,1,64,128]{3,2,1,0:T(8,128)(2,1)}, u32[]{:S(2)}, u32[]{:S(2)}) collective-permute-start(bf16[3,1,64,128]{3,2,1,0:T(8,128)(2,1)} %get-tuple-element.36), channel_id=1, source_target_pairs={{2,0},{4,2},{6,4},{8,6},{10,8},{12,10},{14,12},{16,14},{18,16},{20... | collective-permute-start | bytes 147464 | tf_op jit(solution)/shard_map/ppermute | solution.py:17
  14.8 80.3 %collective-permute-start.5 = (bf16[1,64,128]{2,1,0:T(8,128)(2,1)}, bf16[1,64,128]{2,1,0:T(8,128)(2,1)S(1)}, u32[]{:S(2)}, u32[]{:S(2)}) collective-permute-start(bf16[1,64,128]{2,1,0:T(8,128)(2,1)} %get-tuple-element.79), channel_id=1, source_target_pairs={{2,0},{4,2},{6,4},{8,6},{10,8},{12,10},{14,12},{16,14},{18,16},{20... | collective-permute-start | bytes 49160 | tf_op jit(solution)/shard_map/ppermute | solution.py:17
  15.5 78.9 %collective-permute-start.4 = (bf16[1,64,128]{2,1,0:T(8,128)(2,1)}, bf16[1,64,128]{2,1,0:T(8,128)(2,1)}, u32[]{:S(2)}, u32[]{:S(2)}) collective-permute-start(bf16[1,64,128]{2,1,0:T(8,128)(2,1)} %get-tuple-element.80), channel_id=1, source_target_pairs={{0,2},{2,4},{4,6},{6,8},{8,10},{10,12},{12,14},{14,16},{16,18},{18... | collective-permute-start | bytes 49160 | tf_op jit(solution)/shard_map/ppermute | solution.py:16
  15.5 2.0 copy-start.65
  40.1 41.7 %copy-start.38 = (bf16[128,256]{1,0:T(8,128)(2,1)}, bf16[128,256]{1,0:T(8,128)(2,1)S(1)}, u32[]{:S(2)}) copy-start(bf16[128,256]{1,0:T(8,128)(2,1)S(1)} %copy.83) | copy-start | bytes 196612
  41.6 40.3 %copy-start.41 = (bf16[256,128]{0,1:T(8,128)(2,1)S(1)}, bf16[256,128]{0,1:T(8,128)(2,1)}, u32[]{:S(2)}) copy-start(bf16[256,128]{0,1:T(8,128)(2,1)} %copy.127) | copy-start | bytes 196612
  83.4 19.2 %copy-start.21 = (bf16[128,128]{1,0:T(8,128)(2,1)}, bf16[128,128]{1,0:T(8,128)(2,1)S(1)}, u32[]{:S(2)}) copy-start(bf16[128,128]{1,0:T(8,128)(2,1)S(1)} %mul.1099) | copy-start | bytes 98308
  83.6 1.0 copy-start.13
  83.8 18.4 %copy-start.23 = (bf16[128,128]{1,0:T(8,128)(2,1)}, bf16[128,128]{1,0:T(8,128)(2,1)S(1)}, u32[]{:S(2)}) copy-start(bf16[128,128]{1,0:T(8,128)(2,1)S(1)} %mul.1087) | copy-start | bytes 98308
  84.4 1.0 copy-start.12
  84.6 1.0 copy-start.11
  85.4 1.0 copy-start.10
  85.6 1.0 copy-start.9
  85.8 18.1 %copy-start.25 = (bf16[128,128]{1,0:T(8,128)(2,1)}, bf16[128,128]{1,0:T(8,128)(2,1)S(1)}, u32[]{:S(2)}) copy-start(bf16[128,128]{1,0:T(8,128)(2,1)S(1)} %mul.1063) | copy-start | bytes 98308
  86.3 1.0 copy-start.8
  86.5 1.0 copy-start.7
  86.7 16.8 %copy-start.27 = (bf16[128,128]{1,0:T(8,128)(2,1)}, bf16[128,128]{1,0:T(8,128)(2,1)S(1)}, u32[]{:S(2)}) copy-start(bf16[128,128]{1,0:T(8,128)(2,1)S(1)} %mul.1051) | copy-start | bytes 98308
  87.3 1.0 copy-start.6
  88.7 16.6 %copy-start.29 = (bf16[128,128]{1,0:T(8,128)(2,1)}, bf16[128,128]{1,0:T(8,128)(2,1)S(1)}, u32[]{:S(2)}) copy-start(bf16[128,128]{1,0:T(8,128)(2,1)S(1)} %mul.1027) | copy-start | bytes 98308
  89.8 15.1 %copy-start.19 = (bf16[128,128]{1,0:T(8,128)(2,1)}, bf16[128,128]{1,0:T(8,128)(2,1)S(1)}, u32[]{:S(2)}) copy-start(bf16[128,128]{1,0:T(8,128)(2,1)S(1)} %mul.1015) | copy-start | bytes 98308
  90.6 16.0 %copy-start.17 = (bf16[128,128]{1,0:T(8,128)(2,1)}, bf16[128,128]{1,0:T(8,128)(2,1)S(1)}, u32[]{:S(2)}) copy-start(bf16[128,128]{1,0:T(8,128)(2,1)S(1)} %mul.1035) | copy-start | bytes 98308
  95.9 3.8 %collective-permute-start.6 = (bf16[6,1,128]{2,1,0:T(2,128)(2,1)S(1)}, bf16[6,1,128]{2,1,0:T(2,128)(2,1)S(1)}, u32[]{:S(2)}, u32[]{:S(2)}) collective-permute-start(bf16[6,1,128]{2,1,0:T(2,128)(2,1)S(1)} %get-tuple-element.74), channel_id=1, source_target_pairs={{1,0},{0,1},{3,2},{2,3},{5,4},{4,5},{7,6},{6,7},{9,8},{8,9},{11,10... | collective-permute-start | bytes 4616 | tf_op jit(solution)/shard_map/ppermute | solution.py:17
  98.2 3.6 %collective-permute-start.7 = (bf16[6,1,128]{2,1,0:T(2,128)(2,1)S(1)}, bf16[6,1,128]{2,1,0:T(2,128)(2,1)S(1)}, u32[]{:S(2)}, u32[]{:S(2)}) collective-permute-start(bf16[6,1,128]{2,1,0:T(2,128)(2,1)S(1)} %get-tuple-element.75), channel_id=1, source_target_pairs={{0,1},{1,0},{2,3},{3,2},{4,5},{5,4},{6,7},{7,6},{8,9},{9,8},{10,11... | collective-permute-start | bytes 4616 | tf_op jit(solution)/shard_map/ppermute | solution.py:16
  111.3 2.3 copy-start.39
  111.5 2.1 copy-start.67
  111.5 6.7 %collective-permute-start.3 = (bf16[3,6,1,128]{3,2,1,0:T(2,128)(2,1)S(1)}, bf16[3,6,1,128]{3,2,1,0:T(2,128)(2,1)S(1)}, u32[]{:S(2)}, u32[]{:S(2)}) collective-permute-start(bf16[3,6,1,128]{3,2,1,0:T(2,128)(2,1)S(1)} %get-tuple-element.23), channel_id=1, source_target_pairs={{1,0},{0,1},{3,2},{2,3},{5,4},{4,5},{7,6},{6,7},{9,8},{8,9},{11,10... | collective-permute-start | bytes 13832 | tf_op jit(solution)/shard_map/ppermute | solution.py:17
  111.7 7.6 %collective-permute-start.2 = (bf16[3,6,1,128]{3,2,1,0:T(2,128)(2,1)S(1)}, bf16[3,6,1,128]{3,2,1,0:T(2,128)(2,1)S(1)}, u32[]{:S(2)}, u32[]{:S(2)}) collective-permute-start(bf16[3,6,1,128]{3,2,1,0:T(2,128)(2,1)S(1)} %get-tuple-element.22), channel_id=1, source_target_pairs={{0,1},{1,0},{2,3},{3,2},{4,5},{5,4},{6,7},{7,6},{8,9},{9,8},{10,11... | collective-permute-start | bytes 13832 | tf_op jit(solution)/shard_map/ppermute | solution.py:16
  (49 other events, 37.5 us)
Sparse Core Ops, SparseCore 0:
  167.0 122.5 all-reduce.1
where the time goes:
time: 302 us; the launch traced here: 298 us
  waiting for transfers between devices  121 us (40%)
  local copies, waits for them, and re-layouts  75.9 us (25%)
  blocking collectives  38.9 us (13%)
  matrix products  27.2 us (9%)
  between operations  15.5 us (5%)
  starting transfers between devices  10.6 us (4%)
  other arithmetic  9.07 us (3%)
    psum x1, waiting for transfers between devices, shards(): kernel_sum, bias_sum = lax.psum((kernel_part, bias_part), ('gx', 'gy'))  118 us
    psum x1, blocking collectives, shards(): kernel_sum, bias_sum = lax.psum((kernel_part, bias_part), ('gx', 'gy'))  38.9 us
    unnamed x172, local copies, waits for them, and re-layouts  28 us
    mul x54, local copies, waits for them, and re-layouts, shards(): block_mask[:, None, :, None] * tap_w[None, :, :, :]  19.8 us
    dot_general x27, matrix products, shards(): lax.dot_general(moved, slope_rows, (((0,), (0,)), ((), ())), preferred_el...  17 us
    another operation x28, local copies, waits for them, and re-layouts, shards(): kernel_part = jnp.stack(kernel_rows).reshape(3, 3, 3, group_width, channels)  13.5 us
    another operation x27, local copies, waits for them, and re-layouts, shards(): padded[depth, tap_x:tap_x + width_x, tap_y:tap_y + width_y, :]  10.7 us
    ppermute x4, starting transfers between devices, padded_2(): after = lax.ppermute(initial, axis, down)  8.13 us
  transfers between devices with their start and end apart: 9, of which 3 were waited for; matrix products, arithmetic and copies ran while one was open for 17% of the time, Pallas kernels for 0%

commit v1 on v0

v1 whole, which is shorter than its diff:
```python
import functools

import jax
import jax.numpy as jnp
import numpy as np
from jax import lax
from jax.experimental import pallas as pl
from jax.experimental.pallas import tpu as pltpu
from jax.sharding import PartitionSpec as P

GROUPS = 8
MESH = pl.DeviceIdType.MESH
LOW_X = 4
LOW_Y = 2
PARTS = LOW_X * LOW_Y
F32 = jnp.float32
BF16 = jnp.bfloat16


def kernel_body(
    nx, ny, scale, chunk,
    planes_hbm, kernel_hbm, bias_ref, cot_hbm,
    out_hbm, grad_hbm, sums_hbm,
    planes, taps, cot, edges, edge_halo, cot_halo, planes_halo,
    weights, weights_back, planes_t, cot_views, planes_views, out_v, grad_v,
    part, recv_a, recv_b, total,
    local_sem, halo_send, halo_recv, a_send, a_recv, b_send, b_recv, c_send, c_recv,
):
    depth, wx, wy, ch = planes.shape
    cells = wx * wy
    gw = ch // GROUPS
    gx = lax.axis_index("gx")
    gy = lax.axis_index("gy")
    nb = (nx // LOW_X) * (ny // LOW_Y)
    ia = (gx % LOW_X) * LOW_Y + gy % LOW_Y
    ib = (gx // LOW_X) * (ny // LOW_Y) + gy // LOW_Y

    def peer_a(k):
        j = (ia + k) % PARTS
        return j, ((gx // LOW_X) * LOW_X + j // LOW_Y, (gy // LOW_Y) * LOW_Y + j % LOW_Y)

    def peer_b(k):
        j = (ib + k) % nb
        high_y = ny // LOW_Y
        return ((j // high_y) * LOW_X + gx % LOW_X, (j % high_y) * LOW_Y + gy % LOW_Y)

    def near(dx, dy):
        return ((gx + dx + nx) % nx, (gy + dy + ny) % ny)

    partners = [peer_a(k)[1] for k in range(1, PARTS)] + [peer_b(k) for k in range(1, nb)]
    for dy in ((0, 1) if ny == 2 else (-1, 0, 1)):
        for dx in (-1, 0, 1):
            if (dx, dy) != (0, 0):
                partners.append(near(dx, dy))
    barrier = pltpu.get_barrier_semaphore()
    for where in partners:
        pl.semaphore_signal(barrier, inc=1, device_id=where, device_id_type=MESH)

    in_cot = pltpu.make_async_copy(cot_hbm, cot, local_sem.at[0])
    in_planes = pltpu.make_async_copy(planes_hbm, planes, local_sem.at[1])
    in_taps = pltpu.make_async_copy(kernel_hbm, taps, local_sem.at[2])
    in_cot.start()
    in_planes.start()
    in_taps.start()
    in_cot.wait()
    in_planes.wait()

    rows = [(planes, (z, x)) for z in range(depth) for x in range(wx)] + [(cot, (x,)) for x in range(wx)]
    lane_row = lax.broadcasted_iota(jnp.int32, (16, ch), 0)
    low = jnp.zeros((16, ch), F32)
    high = jnp.zeros((16, ch), F32)
    for r, (ref, at) in enumerate(rows):
        first = ref[at + (slice(0, 16),)].astype(F32)[0:1]
        last = ref[at + (slice(wy - 16, wy),)].astype(F32)[15:16]
        low = jnp.where(lane_row == r, first, low)
        high = jnp.where(lane_row == r, last, high)
    edges[0] = low.astype(BF16)
    edges[1] = high.astype(BF16)

    pl.semaphore_wait(barrier, len(partners))

    def remote(src, dst, send, recv, where):
        copy = pltpu.make_async_remote_copy(
            src_ref=src, dst_ref=dst, send_sem=send, recv_sem=recv, device_id=where, device_id_type=MESH
        )
        copy.start()
        return copy

    cot_copies = [
        remote(cot.at[0], cot_halo.at[1], halo_send.at[0], halo_recv.at[0], near(-1, 0)),
        remote(cot.at[wx - 1], cot_halo.at[0], halo_send.at[1], halo_recv.at[1], near(1, 0)),
    ]
    number = 2
    for side, dy in ((1, -1), (0, 1)):
        for dx in (-1, 0, 1):
            cot_copies.append(
                remote(edges.at[1 - side], edge_halo.at[side, 1 - dx], halo_send.at[number], halo_recv.at[number], near(dx, dy))
            )
            number += 1
    planes_copies = [
        remote(planes.at[:, 0], planes_halo.at[1], halo_send.at[8], halo_recv.at[8], near(-1, 0)),
        remote(planes.at[:, wx - 1], planes_halo.at[0], halo_send.at[9], halo_recv.at[9], near(1, 0)),
    ]

    in_taps.wait()
    row_group = lax.broadcasted_iota(jnp.int32, (ch, ch), 0) // gw
    col_group = lax.broadcasted_iota(jnp.int32, (ch, ch), 1) // gw
    mask = row_group == col_group
    mask_w = jnp.where(mask, 1.0, 0.0).astype(BF16)
    for z in range(depth):
        planes_t[z * ch : (z + 1) * ch, :] = planes[z].reshape(cells, ch).astype(F32).T.astype(BF16)
        for a in range(3):
            for b in range(3):
                tile = jnp.concatenate([taps[z, a, b]] * GROUPS, axis=0) * mask_w
                weights[z, a, b * ch : (b + 1) * ch, :] = tile
                weights_back[a, z * ch : (z + 1) * ch, (2 - b) * ch : (3 - b) * ch] = tile
    spread = jnp.sum(cot[...].reshape(cells, ch).astype(F32), axis=0, keepdims=True)
    whole_row = lax.broadcasted_iota(jnp.int32, (wy, ch), 0)

    def views(target, row, value, left, right):
        value32 = value.astype(F32)
        here = slice(row * wy, (row + 1) * wy)
        target[here, ch : 2 * ch] = value
        target[here, 0:ch] = jnp.where(whole_row == 0, left, pltpu.roll(value32, 1, 0)).astype(BF16)
        target[here, 2 * ch : 3 * ch] = jnp.where(whole_row == wy - 1, right, pltpu.roll(value32, wy - 1, 0)).astype(BF16)

    def side_of(row):
        if row == 0:
            return 0, wx - 1
        if row == wx + 1:
            return 2, 0
        return 1, row - 1

    for copy in cot_copies:
        copy.wait_recv()
    halo32 = [[edge_halo[s, o].astype(F32) for o in range(3)] for s in range(2)]
    for row in range(wx + 2):
        origin, x = side_of(row)
        value = cot_halo[0] if row == 0 else cot_halo[1] if row == wx + 1 else cot[x]
        r = depth * wx + x
        views(cot_views, row, value, halo32[0][origin][r : r + 1], halo32[1][origin][r : r + 1])

    def put(row, value):
        part[row // chunk, row % chunk : row % chunk + 8, :] = value

    for a in range(3):
        full = jnp.dot(
            planes_t[...], cot_views[(2 - a) * wy : (2 - a) * wy + cells, :], preferred_element_type=F32
        )
        for z in range(depth):
            for b in range(3):
                block = full[z * ch : (z + 1) * ch, (2 - b) * ch : (3 - b) * ch]
                block = jnp.where(mask, block, 0.0).reshape(GROUPS, gw, ch).sum(axis=0)
                start = ((z * 3 + a) * 3 + b) * gw
                put(start, block[0:8])
                put(start + 8, block[8:16])
    base = depth * 9 * gw
    put(base, jnp.broadcast_to(spread, (8, ch)))
    for row in range(base + 8, PARTS * chunk, 8):
        put(row, jnp.zeros((8, ch), F32))

    a_copies = []
    for k in range(1, PARTS):
        j, where = peer_a(k)
        a_copies.append(remote(part.at[j], recv_a.at[k - 1], a_send.at[k - 1], a_recv.at[k - 1], where))

    for copy in planes_copies:
        copy.wait_recv()
    for z in range(depth):
        for row in range(wx + 2):
            origin, x = side_of(row)
            value = planes_halo[0, z] if row == 0 else planes_halo[1, z] if row == wx + 1 else planes[z, x]
            r = z * wx + x
            views(planes_views.at[z], row, value, halo32[0][origin][r : r + 1], halo32[1][origin][r : r + 1])
    forward = jnp.zeros((cells, ch), F32)
    for z in range(depth):
        for a in range(3):
            forward = forward + jnp.dot(
                planes_views[z, a * wy : a * wy + cells, :], weights[z, a], preferred_element_type=F32
            )
    out_v[...] = (forward + bias_ref[...]).astype(BF16).reshape(wx, wy, ch)
    put_out = pltpu.make_async_copy(out_v, out_hbm, local_sem.at[3])
    put_out.start()

    for copy in a_copies:
        copy.wait_recv()
    reduced = part[ia]
    for k in range(PARTS - 1):
        reduced = reduced + recv_a[k]
    recv_b[ib] = reduced
    b_copies = []
    for k in range(1, nb):
        b_copies.append(remote(recv_b.at[ib], recv_b.at[ib], b_send.at[k - 1], b_recv.at[k - 1], peer_b(k)))

    slopes = jnp.zeros((cells, depth * ch), F32)
    for a in range(3):
        slopes = slopes + lax.dot_general(
            cot_views[(2 - a) * wy : (2 - a) * wy + cells, :],
            weights_back[a],
            (((1,), (1,)), ((), ())),
            preferred_element_type=F32,
        )
    for z in range(depth):
        grad_v[z] = slopes[:, z * ch : (z + 1) * ch].astype(BF16).reshape(wx, wy, ch)
    put_grad = pltpu.make_async_copy(grad_v, grad_hbm, local_sem.at[4])
    put_grad.start()

    for copy in b_copies:
        copy.wait_recv()
    value = recv_b[0]
    for k in range(1, nb):
        value = value + recv_b[k]
    total[...] = value * scale
    c_copies = []
    for k in range(1, PARTS):
        _, where = peer_a(k)
        c_copies.append(remote(total, sums_hbm.at[ia], c_send.at[k - 1], c_recv.at[k - 1], where))
    put_sum = pltpu.make_async_copy(total, sums_hbm.at[ia], local_sem.at[5])
    put_sum.start()

    for copy in cot_copies + planes_copies + a_copies + b_copies:
        copy.wait_send()
    put_out.wait()
    put_grad.wait()
    put_sum.wait()
    for copy in c_copies:
        copy.wait()


def shards(nx, ny, planes, kernel, bias, cotangent):
    depth, wx, wy, ch = planes.shape
    cells = wx * wy
    gw = ch // GROUPS
    nb = (nx // LOW_X) * (ny // LOW_Y)
    needed = depth * 9 * gw + 8
    chunk = -(-needed // (PARTS * 8)) * 8
    scale = np.float32(1.0) / np.sqrt(np.float32(cells * nx * ny))
    dma = pltpu.SemaphoreType.DMA
    any_space = pl.BlockSpec(memory_space=pl.ANY)
    out, grad, sums = pl.pallas_call(
        functools.partial(kernel_body, nx, ny, scale, chunk),
        out_shape=(
            jax.ShapeDtypeStruct((wx, wy, ch), BF16),
            jax.ShapeDtypeStruct((depth, wx, wy, ch), BF16),
            jax.ShapeDtypeStruct((PARTS, chunk, ch), F32),
        ),
        in_specs=[any_space, any_space, pl.BlockSpec(memory_space=pltpu.VMEM), any_space],
        out_specs=(any_space, any_space, any_space),
        scratch_shapes=[
            pltpu.VMEM((depth, wx, wy, ch), BF16),
            pltpu.VMEM((depth, 3, 3, gw, ch), BF16),
            pltpu.VMEM((wx, wy, ch), BF16),
            pltpu.VMEM((2, 16, ch), BF16),
            pltpu.VMEM((2, 3, 16, ch), BF16),
            pltpu.VMEM((2, wy, ch), BF16),
            pltpu.VMEM((2, depth, wy, ch), BF16),
            pltpu.VMEM((depth, 3, 3 * ch, ch), BF16),
            pltpu.VMEM((3, depth * ch, 3 * ch), BF16),
            pltpu.VMEM((depth * ch, cells), BF16),
            pltpu.VMEM(((wx + 2) * wy, 3 * ch), BF16),
            pltpu.VMEM((depth, (wx + 2) * wy, 3 * ch), BF16),
            pltpu.VMEM((wx, wy, ch), BF16),
            pltpu.VMEM((depth, wx, wy, ch), BF16),
            pltpu.VMEM((PARTS, chunk, ch), F32),
            pltpu.VMEM((PARTS - 1, chunk, ch), F32),
            pltpu.VMEM((nb, chunk, ch), F32),
            pltpu.VMEM((chunk, ch), F32),
            dma((6,)), dma((10,)), dma((10,)),
            dma((PARTS - 1,)), dma((PARTS - 1,)),
            dma((max(nb - 1, 1),)), dma((max(nb - 1, 1),)),
            dma((PARTS - 1,)), dma((PARTS - 1,)),
        ],
        compiler_params=pltpu.CompilerParams(
            collective_id=0, has_side_effects=True, vmem_limit_bytes=32 * 1024 * 1024
        ),
    )(planes, kernel, bias.reshape(1, ch), cotangent)
    flat = sums.reshape(PARTS * chunk, ch)
    base = depth * 9 * gw
    return out, grad, flat[:base].reshape(kernel.shape), flat[base]


def solution(mesh):
    in_specs = (P(None, "gx", "gy", None), P(), P(), P("gx", "gy", None))
    out_specs = (P("gx", "gy", None), P(None, "gx", "gy", None), P(), P())
    body = functools.partial(shards, mesh.shape["gx"], mesh.shape["gy"])
    return jax.shard_map(body, mesh=mesh, in_specs=in_specs, out_specs=out_specs, check_vma=False)
```

time: 302 us -> 29.1 us (0.10); the launches traced: 298 us -> 28.8 us
  waiting for transfers between devices: 121 us -> 0 us
  local copies, waits for them, and re-layouts: 75.9 us -> 5.83 us
  blocking collectives: 38.9 us -> 0 us
  matrix products: 27.2 us -> 0 us
  Pallas kernels: 0 us -> 22.4 us
  between operations: 15.5 us -> 0.65 us
  starting transfers between devices: 10.6 us -> 0 us
  other arithmetic: 9.07 us -> 0 us
    psum x1 -> x0, waiting for transfers between devices: 118 us -> none  [shards(): kernel_sum, bias_sum = lax.psum((kernel_part, bias_part), ('gx', 'gy'))]
    psum x1 -> x0, blocking collectives: 38.9 us -> none  [shards(): kernel_sum, bias_sum = lax.psum((kernel_part, bias_part), ('gx', 'gy'))]
    dot_general x81 -> x0, matrix products: 27.2 us -> none  [the longest x27 17 us: shards(): lax.dot_general(moved, slope_rows, (((0,), (0,)), ((), ())), preferred_el...]
    another operation x55 -> x0, local copies, waits for them, and re-layouts: 24.2 us -> none  [the longest x28 13.5 us: shards(): kernel_part = jnp.stack(kernel_rows).reshape(3, 3, 3, group_width, channels)]
    unnamed x172 -> x10, local copies, waits for them, and re-layouts: 28 us -> 4.62 us
    pallas_call x0 -> x1, Pallas kernels: none -> 22.4 us  [shards(): pl.pallas_call(functools.partial(kernel_body, nx, ny, scale, chunk), out_...]
    mul x54 -> x0, local copies, waits for them, and re-layouts: 19.8 us -> none  [shards(): block_mask[:, None, :, None] * tap_w[None, :, :, :]]
    ppermute x8 -> x0, starting transfers between devices: 10.6 us -> none  [the longest x4 8.13 us: padded_2(): after = lax.ppermute(initial, axis, down)]
  transfers between devices with their start and end apart: 9 -> 0, of which waited for: 3 -> 0; matrix products, arithmetic and copies ran while one was open for 17% -> 0% of each run, Pallas kernels for 0% -> 0%
where the time goes in v1:
time: 29.1 us; the launch traced here: 28.8 us
  Pallas kernels  22.4 us (77%)
  local copies, waits for them, and re-layouts  5.83 us (20%)
  between operations  0.65 us (2%)
    pallas_call x1, Pallas kernels, shards(): pl.pallas_call(functools.partial(kernel_body, nx, ny, scale, chunk), out_...  22.4 us
    unnamed x10, local copies, waits for them, and re-layouts  4.62 us
    slice x1, local copies, waits for them, and re-layouts, shards(): return (out, grad, flat[:base].reshape(kernel.shape), flat[base])  0.7 us

profile of v1, /device:TPU:0, one launch (start us, length us, event | category | flops | bytes accessed | tf_op | source)
XLA Modules:
  0.0 28.8 jit_solution(17185285963007689552)
XLA Ops:
  0.6 0.0 copy-start.3
  0.6 0.6 %copy-done.3 = f32[128]{0:T(128)S(1)} copy-done((f32[128]{0:T(128)S(1)}, f32[128]{0:T(128)}, u32[]{:S(2)}) %copy-start.3) | copy-done | bytes 536
  1.3 0.0 copy-start
  1.3 0.9 %copy-done = bf16[3,4,64,128]{3,2,1,0:T(8,128)(2,1)S(1)} copy-done((bf16[3,4,64,128]{3,2,1,0:T(8,128)(2,1)S(1)}, bf16[3,4,64,128]{3,2,1,0:T(8,128)(2,1)}, u32[]{:S(2)}) %copy-start) | copy-done | bytes 196632
  2.2 0.0 copy-start.1
  2.2 0.9 %copy-done.1 = bf16[3,3,3,16,128]{4,3,2,1,0:T(8,128)(2,1)S(1)} copy-done((bf16[3,3,3,16,128]{4,3,2,1,0:T(8,128)(2,1)S(1)}, bf16[3,3,3,16,128]{4,3,2,1,0:T(8,128)(2,1)}, u32[]{:S(2)}) %copy-start.1) | copy-done | bytes 110616
  3.1 0.0 copy-start.2
  3.1 0.8 %copy-done.2 = bf16[4,64,128]{2,1,0:T(8,128)(2,1)S(1)} copy-done((bf16[4,64,128]{2,1,0:T(8,128)(2,1)S(1)}, bf16[4,64,128]{2,1,0:T(8,128)(2,1)}, u32[]{:S(2)}) %copy-start.2) | copy-done | bytes 65560
  4.0 22.4 %shard_map.75 = (bf16[4,64,128]{2,1,0:T(8,128)(2,1)S(1)}, bf16[3,4,64,128]{3,2,1,0:T(8,128)(2,1)S(1)}, f32[8,56,128]{2,1,0:T(8,128)S(1)}) custom-call(bf16[3,4,64,128]{3,2,1,0:T(8,128)(2,1)S(1)} %copy-done, bf16[3,3,3,16,128]{4,3,2,1,0:T(8,128)(2,1)S(1)} %copy-done.1, f32[1,128]{1,0:T(1,128)S(1)} %bitcast.7, bf16[4,64,128]{2,1,0:T(8,128)(2,1)S(1)} %copy-done.2), custom_call_target="tpu_custom_call" | custom-call | tf_op jit(solution)/shard_map/pallas_call | solution.py:240
  26.3 0.5 %slice_bitcast_fusion = f32[128]{0:T(128)} fusion(f32[448,128]{1,0:T(8,128)S(1)} %bitcast.5), kind=kLoop, calls=%fused_computation | loop fusion | bytes 1024 | tf_op jit(solution)/shard_map/squeeze | solution.py:279
  26.8 0.7 %slice.8 = f32[432,128]{1,0:T(8,128)} slice(f32[448,128]{1,0:T(8,128)S(1)} %bitcast.6), slice={[0:432], [0:128]} | slice | bytes 442368 | tf_op jit(solution)/shard_map/slice | solution.py:279
  27.5 0.6 %copy.10 = bf16[4,64,128]{2,1,0:T(8,128)(2,1)} copy(bf16[4,64,128]{2,1,0:T(8,128)(2,1)S(1)} %get-tuple-element.14) | data formatting | bytes 131072
  28.2 0.7 %copy.11 = bf16[3,4,64,128]{3,2,1,0:T(8,128)(2,1)} copy(bf16[3,4,64,128]{3,2,1,0:T(8,128)(2,1)S(1)} %get-tuple-element.15) | data formatting | bytes 393216
Async XLA Ops:
  0.6 0.7 %copy-start.3 = (f32[128]{0:T(128)S(1)}, f32[128]{0:T(128)}, u32[]{:S(2)}) copy-start(f32[128]{0:T(128)} %param.6) | copy-start | bytes 1540
  1.3 0.9 %copy-start = (bf16[3,4,64,128]{3,2,1,0:T(8,128)(2,1)S(1)}, bf16[3,4,64,128]{3,2,1,0:T(8,128)(2,1)}, u32[]{:S(2)}) copy-start(bf16[3,4,64,128]{3,2,1,0:T(8,128)(2,1)} %planes_hbm.1) | copy-start | bytes 589828
  2.2 0.9 %copy-start.1 = (bf16[3,3,3,16,128]{4,3,2,1,0:T(8,128)(2,1)S(1)}, bf16[3,3,3,16,128]{4,3,2,1,0:T(8,128)(2,1)}, u32[]{:S(2)}) copy-start(bf16[3,3,3,16,128]{4,3,2,1,0:T(8,128)(2,1)} %kernel_hbm.1) | copy-start | bytes 331780
  3.1 0.8 %copy-start.2 = (bf16[4,64,128]{2,1,0:T(8,128)(2,1)S(1)}, bf16[4,64,128]{2,1,0:T(8,128)(2,1)}, u32[]{:S(2)}) copy-start(bf16[4,64,128]{2,1,0:T(8,128)(2,1)} %cot_hbm.1) | copy-start | bytes 196612

commit v2 on v1

--- a/solution.py
+++ b/solution.py
@@ -19,11 +19,11 @@
 
 def kernel_body(
     nx, ny, scale, chunk,
-    planes_hbm, kernel_hbm, bias_ref, cot_hbm,
-    out_hbm, grad_hbm, sums_hbm,
-    planes, taps, cot, edges, edge_halo, cot_halo, planes_halo,
-    weights, weights_back, planes_t, cot_views, planes_views, out_v, grad_v,
-    part, recv_a, recv_b, total,
+    planes_hbm, kernel_hbm, bias_hbm, cot_hbm,
+    out_ref, grad_ref, sums_ref,
+    planes, taps, bias, cot, edges, edge_halo, cot_halo, planes_halo,
+    weights, weights_back, planes_t, cot_views, planes_views,
+    part, recv_a, recv_b,
     local_sem, halo_send, halo_recv, a_send, a_recv, b_send, b_recv, c_send, c_recv,
 ):
     depth, wx, wy, ch = planes.shape
@@ -62,6 +62,8 @@
     in_cot.start()
     in_planes.start()
     in_taps.start()
+    in_bias = pltpu.make_async_copy(bias_hbm, bias, local_sem.at[3])
+    in_bias.start()
     in_cot.wait()
     in_planes.wait()
 
@@ -103,6 +105,7 @@
     ]
 
     in_taps.wait()
+    in_bias.wait()
     row_group = lax.broadcasted_iota(jnp.int32, (ch, ch), 0) // gw
     col_group = lax.broadcasted_iota(jnp.int32, (ch, ch), 1) // gw
     mask = row_group == col_group
@@ -178,9 +181,7 @@
             forward = forward + jnp.dot(
                 planes_views[z, a * wy : a * wy + cells, :], weights[z, a], preferred_element_type=F32
             )
-    out_v[...] = (forward + bias_ref[...]).astype(BF16).reshape(wx, wy, ch)
-    put_out = pltpu.make_async_copy(out_v, out_hbm, local_sem.at[3])
-    put_out.start()
+    out_ref[...] = (forward + bias[...]).astype(BF16).reshape(wx, wy, ch)
 
     for copy in a_copies:
         copy.wait_recv()
@@ -201,29 +202,36 @@
             preferred_element_type=F32,
         )
     for z in range(depth):
-        grad_v[z] = slopes[:, z * ch : (z + 1) * ch].astype(BF16).reshape(wx, wy, ch)
-    put_grad = pltpu.make_async_copy(grad_v, grad_hbm, local_sem.at[4])
-    put_grad.start()
+        grad_ref[z] = slopes[:, z * ch : (z + 1) * ch].astype(BF16).reshape(wx, wy, ch)
 
     for copy in b_copies:
         copy.wait_recv()
     value = recv_b[0]
     for k in range(1, nb):
         value = value + recv_b[k]
-    total[...] = value * scale
+    sums_ref[ia] = value * scale
     c_copies = []
     for k in range(1, PARTS):
         _, where = peer_a(k)
-        c_copies.append(remote(total, sums_hbm.at[ia], c_send.at[k - 1], c_recv.at[k - 1], where))
-    put_sum = pltpu.make_async_copy(total, sums_hbm.at[ia], local_sem.at[5])
-    put_sum.start()
+        c_copies.append(remote(sums_ref.at[ia], sums_ref.at[ia], c_send.at[k - 1], c_recv.at[k - 1], where))
 
     for copy in cot_copies + planes_copies + a_copies + b_copies:
         copy.wait_send()
-    put_out.wait()
-    put_grad.wait()
-    put_sum.wait()
     for copy in c_copies:
+        copy.wait()
+
+
+def place_body(out_from, grad_from, sums, out_to, grad_to, kernel_to, bias_to, sem):
+    base = kernel_to.shape[0]
+    copies = [
+        pltpu.make_async_copy(grad_from, grad_to, sem.at[0]),
+        pltpu.make_async_copy(sums.at[0:base], kernel_to, sem.at[1]),
+        pltpu.make_async_copy(out_from, out_to, sem.at[2]),
+        pltpu.make_async_copy(sums.at[base : base + 1], bias_to, sem.at[3]),
+    ]
+    for copy in copies:
+        copy.start()
+    for copy in copies:
         copy.wait()
 
 
@@ -236,7 +244,8 @@
     chunk = -(-needed // (PARTS * 8)) * 8
     scale = np.float32(1.0) / np.sqrt(np.float32(cells * nx * ny))
     dma = pltpu.SemaphoreType.DMA
-    any_space = pl.BlockSpec(memory_space=pl.ANY)
+    vmem = pl.BlockSpec(memory_space=pltpu.VMEM)
+    hbm = pl.BlockSpec(memory_space=pltpu.HBM)
     out, grad, sums = pl.pallas_call(
         functools.partial(kernel_body, nx, ny, scale, chunk),
         out_shape=(
@@ -244,11 +253,12 @@
             jax.ShapeDtypeStruct((depth, wx, wy, ch), BF16),
             jax.ShapeDtypeStruct((PARTS, chunk, ch), F32),
         ),
-        in_specs=[any_space, any_space, pl.BlockSpec(memory_space=pltpu.VMEM), any_space],
-        out_specs=(any_space, any_space, any_space),
+        in_specs=[hbm, hbm, hbm, hbm],
+        out_specs=(vmem,) * 3,
         scratch_shapes=[
             pltpu.VMEM((depth, wx, wy, ch), BF16),
             pltpu.VMEM((depth, 3, 3, gw, ch), BF16),
+            pltpu.VMEM((1, ch), F32),
             pltpu.VMEM((wx, wy, ch), BF16),
             pltpu.VMEM((2, 16, ch), BF16),
             pltpu.VMEM((2, 3, 16, ch), BF16),
@@ -259,13 +269,10 @@
             pltpu.VMEM((depth * ch, cells), BF16),
             pltpu.VMEM(((wx + 2) * wy, 3 * ch), BF16),
             pltpu.VMEM((depth, (wx + 2) * wy, 3 * ch), BF16),
-            pltpu.VMEM((wx, wy, ch), BF16),
-            pltpu.VMEM((depth, wx, wy, ch), BF16),
             pltpu.VMEM((PARTS, chunk, ch), F32),
             pltpu.VMEM((PARTS - 1, chunk, ch), F32),
             pltpu.VMEM((nb, chunk, ch), F32),
-            pltpu.VMEM((chunk, ch), F32),
-            dma((6,)), dma((10,)), dma((10,)),
+            dma((4,)), dma((10,)), dma((10,)),
             dma((PARTS - 1,)), dma((PARTS - 1,)),
             dma((max(nb - 1, 1),)), dma((max(nb - 1, 1),)),
             dma((PARTS - 1,)), dma((PARTS - 1,)),
@@ -273,10 +280,21 @@
         compiler_params=pltpu.CompilerParams(
             collective_id=0, has_side_effects=True, vmem_limit_bytes=32 * 1024 * 1024
         ),
-    )(planes, kernel, bias.reshape(1, ch), cotangent)
-    flat = sums.reshape(PARTS * chunk, ch)
+    )(*(pltpu.with_memory_space_constraint(x, pltpu.HBM) for x in (planes, kernel, bias.reshape(1, ch), cotangent)))
     base = depth * 9 * gw
-    return out, grad, flat[:base].reshape(kernel.shape), flat[base]
+    out, grad, kernel_grad, bias_grad = pl.pallas_call(
+        place_body,
+        out_shape=(
+            jax.ShapeDtypeStruct(out.shape, BF16),
+            jax.ShapeDtypeStruct(grad.shape, BF16),
+            jax.ShapeDtypeStruct((base, ch), F32),
+            jax.ShapeDtypeStruct((1, ch), F32),
+        ),
+        in_specs=[vmem] * 3,
+        out_specs=(hbm, hbm, hbm, hbm),
+        scratch_shapes=[dma((4,))],
+    )(*(pltpu.with_memory_space_constraint(x, pltpu.VMEM) for x in (out, grad, sums.reshape(PARTS * chunk, ch))))
+    return out, grad, kernel_grad.reshape(kernel.shape), bias_grad.reshape(ch)
 
 
 def solution(mesh):

time: 29.1 us -> 24.2 us (0.83)
  local copies, waits for them, and re-layouts: 5.83 us -> 0 us
  Pallas kernels: 22.4 us -> 23.4 us
    unnamed x10 -> x0, local copies, waits for them, and re-layouts: 4.62 us -> none
    pallas_call x0 -> x1, Pallas kernels: none -> 0.81 us  [shards(): pl.pallas_call(place_body, out_shape=(jax.ShapeDtypeStruct(out.shape, BF1...]
    slice x1 -> x0, local copies, waits for them, and re-layouts: 0.7 us -> none  [shards(): return (out, grad, flat[:base].reshape(kernel.shape), flat[base])]
    squeeze x1 -> x0, local copies, waits for them, and re-layouts: 0.51 us -> none  [shards(): return (out, grad, flat[:base].reshape(kernel.shape), flat[base])]
where the time goes in v2:
time: 24.2 us; the launch traced here: 24.1 us
  Pallas kernels  23.4 us (97%)
  between operations  0.64 us (3%)
    pallas_call x1, Pallas kernels, shards(): pl.pallas_call(functools.partial(kernel_body, nx, ny, scale, chunk), out_...  22.6 us
    pallas_call x1, Pallas kernels, shards(): pl.pallas_call(place_body, out_shape=(jax.ShapeDtypeStruct(out.shape, BF1...  0.81 us

profile of v2, /device:TPU:0, one launch (start us, length us, event | category | flops | bytes accessed | tf_op | source)
XLA Modules:
  0.0 24.1 jit_solution(4027143047457183611)
XLA Ops:
  0.6 22.6 %shard_map.75 = (bf16[4,64,128]{2,1,0:T(8,128)(2,1)S(1)}, bf16[3,4,64,128]{3,2,1,0:T(8,128)(2,1)S(1)}, f32[8,56,128]{2,1,0:T(8,128)S(1)}) custom-call(bf16[3,4,64,128]{3,2,1,0:T(8,128)(2,1)} %planes_hbm.1, bf16[3,3,3,16,128]{4,3,2,1,0:T(8,128)(2,1)} %kernel_hbm.1, f32[1,128]{1,0:T(1,128)} %bitcast.5, bf16[4,64,128]{2,1,0:T(8,128)(2,1)} %cot_hbm.1), custom_call_target="tpu_custom_call" | custom-call | tf_op jit(solution)/shard_map/pallas_call | solution.py:249
  23.2 0.8 %shard_map.76 = (bf16[4,64,128]{2,1,0:T(8,128)(2,1)}, bf16[3,4,64,128]{3,2,1,0:T(8,128)(2,1)}, f32[432,128]{1,0:T(8,128)}, f32[1,128]{1,0:T(1,128)}) custom-call(bf16[4,64,128]{2,1,0:T(8,128)(2,1)S(1)} %get-tuple-element.11.out_from, bf16[3,4,64,128]{3,2,1,0:T(8,128)(2,1)S(1)} %get-tuple-element.12.grad_from, f32[448,128]{1,0:T(8,128)S(1)} %bitcast.4), custom_call_target="tpu_custom_call" | custom-call | tf_op jit(solution)/shard_map/pallas_call | solution.py:285

commit v3 on v2

--- a/solution.py
+++ b/solution.py
@@ -32,30 +32,36 @@
     gx = lax.axis_index("gx")
     gy = lax.axis_index("gy")
     nb = (nx // LOW_X) * (ny // LOW_Y)
-    ia = (gx % LOW_X) * LOW_Y + gy % LOW_Y
-    ib = (gx // LOW_X) * (ny // LOW_Y) + gy // LOW_Y
+    high_y = ny // LOW_Y
+    low_gx, low_gy = lax.rem(gx, LOW_X), lax.rem(gy, LOW_Y)
+    high_gx, high_gy = lax.div(gx, LOW_X), lax.div(gy, LOW_Y)
+    ia = low_gx * LOW_Y + low_gy
+    ib = high_gx * high_y + high_gy
+    peers_a = [None]
+    for k in range(1, PARTS):
+        j = lax.rem(ia + k, PARTS)
+        peers_a.append((j, (high_gx * LOW_X + lax.div(j, LOW_Y), high_gy * LOW_Y + lax.rem(j, LOW_Y))))
+    peers_b = [None]
+    for k in range(1, nb):
+        j = lax.rem(ib + k, nb)
+        peers_b.append((lax.div(j, high_y) * LOW_X + low_gx, lax.rem(j, high_y) * LOW_Y + low_gy))
+    around_x = {-1: lax.rem(gx + nx - 1, nx), 0: gx, 1: lax.rem(gx + 1, nx)}
+    around_y = {-1: lax.rem(gy + ny - 1, ny), 0: gy, 1: lax.rem(gy + 1, ny)}
 
     def peer_a(k):
-        j = (ia + k) % PARTS
-        return j, ((gx // LOW_X) * LOW_X + j // LOW_Y, (gy // LOW_Y) * LOW_Y + j % LOW_Y)
+        return peers_a[k]
 
     def peer_b(k):
-        j = (ib + k) % nb
-        high_y = ny // LOW_Y
-        return ((j // high_y) * LOW_X + gx % LOW_X, (j % high_y) * LOW_Y + gy % LOW_Y)
+        return peers_b[k]
 
     def near(dx, dy):
-        return ((gx + dx + nx) % nx, (gy + dy + ny) % ny)
+        return (around_x[dx], around_y[dy])
 
     partners = [peer_a(k)[1] for k in range(1, PARTS)] + [peer_b(k) for k in range(1, nb)]
     for dy in ((0, 1) if ny == 2 else (-1, 0, 1)):
         for dx in (-1, 0, 1):
             if (dx, dy) != (0, 0):
                 partners.append(near(dx, dy))
-    barrier = pltpu.get_barrier_semaphore()
-    for where in partners:
-        pl.semaphore_signal(barrier, inc=1, device_id=where, device_id_type=MESH)
-
     in_cot = pltpu.make_async_copy(cot_hbm, cot, local_sem.at[0])
     in_planes = pltpu.make_async_copy(planes_hbm, planes, local_sem.at[1])
     in_taps = pltpu.make_async_copy(kernel_hbm, taps, local_sem.at[2])
@@ -64,6 +70,10 @@
     in_taps.start()
     in_bias = pltpu.make_async_copy(bias_hbm, bias, local_sem.at[3])
     in_bias.start()
+    barrier = pltpu.get_barrier_semaphore()
+    for where in partners:
+        pl.semaphore_signal(barrier, inc=1, device_id=where, device_id_type=MESH)
+
     in_cot.wait()
     in_planes.wait()
 
@@ -104,19 +114,12 @@
         remote(planes.at[:, wx - 1], planes_halo.at[0], halo_send.at[9], halo_recv.at[9], near(1, 0)),
     ]
 
-    in_taps.wait()
-    in_bias.wait()
     row_group = lax.broadcasted_iota(jnp.int32, (ch, ch), 0) // gw
     col_group = lax.broadcasted_iota(jnp.int32, (ch, ch), 1) // gw
     mask = row_group == col_group
     mask_w = jnp.where(mask, 1.0, 0.0).astype(BF16)
     for z in range(depth):
         planes_t[z * ch : (z + 1) * ch, :] = planes[z].reshape(cells, ch).astype(F32).T.astype(BF16)
-        for a in range(3):
-            for b in range(3):
-                tile = jnp.concatenate([taps[z, a, b]] * GROUPS, axis=0) * mask_w
-                weights[z, a, b * ch : (b + 1) * ch, :] = tile
-                weights_back[a, z * ch : (z + 1) * ch, (2 - b) * ch : (3 - b) * ch] = tile
     spread = jnp.sum(cot[...].reshape(cells, ch).astype(F32), axis=0, keepdims=True)
     whole_row = lax.broadcasted_iota(jnp.int32, (wy, ch), 0)
 
@@ -162,11 +165,23 @@
     for row in range(base + 8, PARTS * chunk, 8):
         put(row, jnp.zeros((8, ch), F32))
 
-    a_copies = []
-    for k in range(1, PARTS):
-        j, where = peer_a(k)
-        a_copies.append(remote(part.at[j], recv_a.at[k - 1], a_send.at[k - 1], a_recv.at[k - 1], where))
-
+    pieces = [slice(0, 32), slice(32, chunk)]
+    a_copies = [[], []]
+    for h, rows in enumerate(pieces):
+        for k in range(1, PARTS):
+            j, where = peer_a(k)
+            a_copies[h].append(
+                remote(part.at[j, rows], recv_a.at[k - 1, rows], a_send.at[h, k - 1], a_recv.at[h, k - 1], where)
+            )
+
+    in_taps.wait()
+    in_bias.wait()
+    for z in range(depth):
+        for a in range(3):
+            for b in range(3):
+                tile = jnp.concatenate([taps[z, a, b]] * GROUPS, axis=0) * mask_w
+                weights[z, a, b * ch : (b + 1) * ch, :] = tile
+                weights_back[a, z * ch : (z + 1) * ch, (2 - b) * ch : (3 - b) * ch] = tile
     for copy in planes_copies:
         copy.wait_recv()
     for z in range(depth):
@@ -183,15 +198,18 @@
             )
     out_ref[...] = (forward + bias[...]).astype(BF16).reshape(wx, wy, ch)
 
-    for copy in a_copies:
-        copy.wait_recv()
-    reduced = part[ia]
-    for k in range(PARTS - 1):
-        reduced = reduced + recv_a[k]
-    recv_b[ib] = reduced
-    b_copies = []
-    for k in range(1, nb):
-        b_copies.append(remote(recv_b.at[ib], recv_b.at[ib], b_send.at[k - 1], b_recv.at[k - 1], peer_b(k)))
+    b_copies = [[], []]
+    for h, rows in enumerate(pieces):
+        for copy in a_copies[h]:
+            copy.wait_recv()
+        reduced = part[ia, rows]
+        for k in range(PARTS - 1):
+            reduced = reduced + recv_a[k, rows]
+        recv_b[ib, rows] = reduced
+        for k in range(1, nb):
+            b_copies[h].append(
+                remote(recv_b.at[ib, rows], recv_b.at[ib, rows], b_send.at[h, k - 1], b_recv.at[h, k - 1], peer_b(k))
+            )
 
     slopes = jnp.zeros((cells, depth * ch), F32)
     for a in range(3):
@@ -204,18 +222,21 @@
     for z in range(depth):
         grad_ref[z] = slopes[:, z * ch : (z + 1) * ch].astype(BF16).reshape(wx, wy, ch)
 
-    for copy in b_copies:
-        copy.wait_recv()
-    value = recv_b[0]
-    for k in range(1, nb):
-        value = value + recv_b[k]
-    sums_ref[ia] = value * scale
     c_copies = []
-    for k in range(1, PARTS):
-        _, where = peer_a(k)
-        c_copies.append(remote(sums_ref.at[ia], sums_ref.at[ia], c_send.at[k - 1], c_recv.at[k - 1], where))
-
-    for copy in cot_copies + planes_copies + a_copies + b_copies:
+    for h, rows in enumerate(pieces):
+        for copy in b_copies[h]:
+            copy.wait_recv()
+        value = recv_b[0, rows]
+        for k in range(1, nb):
+            value = value + recv_b[k, rows]
+        sums_ref[ia, rows] = value * scale
+        for k in range(1, PARTS):
+            _, where = peer_a(k)
+            c_copies.append(
+                remote(sums_ref.at[ia, rows], sums_ref.at[ia, rows], c_send.at[h, k - 1], c_recv.at[h, k - 1], where)
+            )
+
+    for copy in cot_copies + planes_copies + sum(a_copies + b_copies, []):
         copy.wait_send()
     for copy in c_copies:
         copy.wait()
@@ -273,9 +294,9 @@
             pltpu.VMEM((PARTS - 1, chunk, ch), F32),
             pltpu.VMEM((nb, chunk, ch), F32),
             dma((4,)), dma((10,)), dma((10,)),
-            dma((PARTS - 1,)), dma((PARTS - 1,)),
-            dma((max(nb - 1, 1),)), dma((max(nb - 1, 1),)),
-            dma((PARTS - 1,)), dma((PARTS - 1,)),
+            dma((2, PARTS - 1)), dma((2, PARTS - 1)),
+            dma((2, max(nb - 1, 1))), dma((2, max(nb - 1, 1))),
+            dma((2, PARTS - 1)), dma((2, PARTS - 1)),
         ],
         compiler_params=pltpu.CompilerParams(
             collective_id=0, has_side_effects=True, vmem_limit_bytes=32 * 1024 * 1024

time: 24.2 us -> 24.1 us (level)
  no operation moved by 1% of the time
where the time goes in v3:
time: 24.1 us; the launch traced here: 24 us
  Pallas kernels  23.4 us (97%)
  between operations  0.64 us (3%)
    pallas_call x1, Pallas kernels, shards(): pl.pallas_call(functools.partial(kernel_body, nx, ny, scale, chunk), out_...  22.5 us
    pallas_call x1, Pallas kernels, shards(): pl.pallas_call(place_body, out_shape=(jax.ShapeDtypeStruct(out.shape, BF1...  0.81 us

profile of v3, /device:TPU:0, one launch (start us, length us, event | category | flops | bytes accessed | tf_op | source)
XLA Modules:
  0.0 24.0 jit_solution(4251719068279209736)
XLA Ops:
  0.6 22.5 %shard_map.75 = (bf16[4,64,128]{2,1,0:T(8,128)(2,1)S(1)}, bf16[3,4,64,128]{3,2,1,0:T(8,128)(2,1)S(1)}, f32[8,56,128]{2,1,0:T(8,128)S(1)}) custom-call(bf16[3,4,64,128]{3,2,1,0:T(8,128)(2,1)} %planes_hbm.1, bf16[3,3,3,16,128]{4,3,2,1,0:T(8,128)(2,1)} %kernel_hbm.1, f32[1,128]{1,0:T(1,128)} %bitcast.5, bf16[4,64,128]{2,1,0:T(8,128)(2,1)} %cot_hbm.1), custom_call_target="tpu_custom_call" | custom-call | tf_op jit(solution)/shard_map/pallas_call | solution.py:270
  23.2 0.8 %shard_map.76 = (bf16[4,64,128]{2,1,0:T(8,128)(2,1)}, bf16[3,4,64,128]{3,2,1,0:T(8,128)(2,1)}, f32[432,128]{1,0:T(8,128)}, f32[1,128]{1,0:T(1,128)}) custom-call(bf16[4,64,128]{2,1,0:T(8,128)(2,1)S(1)} %get-tuple-element.11.out_from, bf16[3,4,64,128]{3,2,1,0:T(8,128)(2,1)S(1)} %get-tuple-element.12.grad_from, f32[448,128]{1,0:T(8,128)S(1)} %bitcast.4), custom_call_target="tpu_custom_call" | custom-call | tf_op jit(solution)/shard_map/pallas_call | solution.py:306
